TPU v7x, 128 devices: a whole 4x4x4 slice. The times are simulated.
128 devices in a mesh: row: 16 (over x, y_lo, core), col: 8 (over z, y_hi).
Axes of the slice: x: 4, y: 4 (y_hi: 2, y_lo: 2; y = y_hi * 2 + y_lo), z: 4, core: 2. Of those that a mesh axis runs over, the one named last changes fastest.
Arguments:
- x_blocks: bfloat16 [256, 16, 2, 128, 128], P('row', 'col'), may hold values from -1.796875 to 1.796875
- x_columns: int32 [256, 16, 2], P('row', 'col'), may hold values from 0 to 95, as said below
- kept_columns: int32 [1536, 16], P('row', 'col'), may hold values from 0 to 191, as said below
Outputs:
- result_blocks: float32 [1536, 16, 128, 128], P('row', 'col')
Inputs may be any that keep to these rules, and one draw needn't show every extreme that they name: `x_columns`: the 2 entries of one block row and one group are distinct. `kept_columns`: the 2 entries of one result block row within one column panel are distinct.
All inputs are finite; a program needn't handle non-finite values.
Results may differ from a plain program's by a relative error of at most 0.0003.
Values may be sent and summed in bfloat16 or wider, within the bound.
A program may use at most 320 MiB of HBM per device.

v0:
```python
import jax
import jax.numpy as jnp
from jax import lax
from jax.sharding import PartitionSpec as P


def block_products(a_values, a_cols, b_values, b_cols, kept_columns):
    row_count = a_values.shape[0]
    block_size = a_values.shape[-1]
    width_g = kept_columns.shape[0]
    slots_b = b_values.shape[1] * b_values.shape[2]
    panel_pos = (lax.broadcasted_iota(jnp.int32, b_cols.shape, 1) * width_g + b_cols).reshape(
        row_count, slots_b
    )
    b_flat = b_values.reshape(row_count, slots_b, block_size, block_size)
    onehot = a_cols[:, :, None] == lax.broadcasted_iota(jnp.int32, (1, 1, width_g), 2)
    kept_here = jnp.sum(jnp.where(onehot[:, :, :, None], kept_columns[None, None, :, :], 0), axis=2)
    selector = (kept_here[:, :, :, None] == panel_pos[:, None, None, :]).astype(jnp.bfloat16)
    chosen = jnp.einsum(
        "kesf,kftj->kestj", selector, b_flat, preferred_element_type=jnp.float32
    ).astype(jnp.bfloat16)
    return jnp.einsum("keti,kestj->kesij", a_values, chosen, preferred_element_type=jnp.float32)


def reduce_rows(products, a_cols, width_g):
    pair_count = a_cols.shape[0] * a_cols.shape[1]
    kept_count = products.shape[-3]
    block_size = products.shape[-1]
    targets = a_cols.reshape(pair_count)
    flat = products.reshape(pair_count, kept_count, block_size, block_size)
    zero_sums = jnp.zeros((width_g, kept_count, block_size, block_size), jnp.float32)
    return zero_sums.at[targets].add(flat)


def on_device(x_blocks, x_columns, kept_columns):
    rows_here = x_blocks.shape[0]
    slot_count = x_blocks.shape[2]
    block_size = x_blocks.shape[-1]
    width_g = kept_columns.shape[0]
    n_row = lax.axis_size("row")
    n_col = lax.axis_size("col")
    col_tags = x_columns.astype(jnp.bfloat16)
    relaid = (
        lax.all_to_all(x_blocks, "col", split_axis=0, concat_axis=1, tiled=True),
        lax.all_to_all(col_tags, "col", split_axis=0, concat_axis=1, tiled=True),
    )
    relaid = (
        lax.all_to_all(relaid[0], "row", split_axis=1, concat_axis=0, tiled=True),
        lax.all_to_all(relaid[1], "row", split_axis=1, concat_axis=0, tiled=True),
    )
    gathered = (
        lax.all_gather(relaid[0][:, 0], "col", axis=0, tiled=True),
        lax.all_gather(relaid[1][:, 0], "col", axis=0, tiled=True),
    )
    sub_rows = rows_here // n_col
    a_values = gathered[0].reshape(n_col, n_row, sub_rows, slot_count, block_size, block_size)
    a_values = a_values.transpose(1, 0, 2, 3, 4, 5).reshape(
        n_row * rows_here, slot_count, block_size, block_size
    )
    a_cols = gathered[1].reshape(n_col, n_row, sub_rows, slot_count).transpose(1, 0, 2, 3)
    a_cols = a_cols.reshape(n_row * rows_here, slot_count).astype(jnp.int32)
    b_values = lax.all_gather(x_blocks, "row", axis=0, tiled=True)
    b_tags = lax.all_gather(col_tags, "row", axis=0, tiled=True)
    fresh = block_products(a_values, a_cols, b_values, b_tags.astype(jnp.int32), kept_columns)
    summed = reduce_rows(fresh, a_cols, width_g)
    return summed


def solution(mesh):
    placed = (P("row", "col", None, None, None), P("row", "col", None), P("row", "col"))
    return jax.shard_map(
        on_device,
        mesh=mesh,
        in_specs=placed,
        out_specs=P("row", "col", None, None),
        check_vma=False,
    )
```

profile of v0, /device:TPU:0, one launch (start us, length us, event | category | flops | bytes accessed | tf_op | source)
XLA Modules:
  0.0 803.4 jit_solution(1905037539071177490)
XLA Ops:
  6.5 0.0 all-gather.6.cloned.1.call-start
  6.5 36.5 %all_to_all.66 = bf16[16,2,2,128,128]{4,3,2,1,0:T(8,128)(2,1)S(1)} all-to-all(bf16[16,2,2,128,128]{4,3,2,1,0:T(8,128)(2,1)} %param.3), channel_id=1, replica_groups=mesh['row'=16,'col'=8] {'col'}, dimensions={0} | all-to-all | bytes 4194304 | tf_op jit(solution)/shard_map/all_to_all | solution.py:44
  43.0 0.2 copy.102
  43.2 0.2 copy.103
  43.5 32.4 %all_to_all.67 = bf16[2,16,2,128,128]{4,3,2,0,1:T(8,128)(2,1)} all-to-all(bf16[2,16,2,128,128]{4,3,2,0,1:T(8,128)(2,1)S(1)} %copy.103), channel_id=1, replica_groups=mesh['row'=16,'col'=8] {'row'}, dimensions={1} | all-to-all | bytes 4194304 | tf_op jit(solution)/shard_map/all_to_all | solution.py:48
  75.9 0.0 all-gather.6.cloned.1.call-update
  75.9 0.0 all-gather.4.cloned.1.call-start
  76.0 0.7 all-gather.4.cloned.1.call-update
  76.7 0.8 copy.88
  77.4 0.6 convert_element_type.41
  78.1 3.3 all-to-all-start
  81.4 17.4 %all_gather.13 = bf16[256,2,2]{2,1,0:T(2,128)(2,1)S(1)} all-gather(bf16[16,2,2]{2,1,0:T(2,128)(2,1)} %convert_element_type.41), channel_id=1, replica_groups=mesh['row'=16,'col'=8] {'row'}, dimensions={0}, use_global_device_ids=true | all-gather | bytes 2176 | tf_op jit(solution)/shard_map/all_gather | solution.py:63
  98.8 0.1 copy.99
  98.9 0.1 convert_add_fusion
  99.0 0.0 all-to-all-done
  99.0 0.2 copy.111
  99.2 0.8 copy.112
  100.0 3.5 all-to-all-start.1
  103.5 0.1 copy.100
  103.6 5.8 all-to-all-done.1
  109.4 0.1 copy.92
  109.5 0.1 copy.93
  109.6 0.1 reshape.72
  109.7 24.3 %all-gather = bf16[8,32,2]{1,2,0:T(2,128)(2,1)S(1)} all-gather(bf16[1,32,2]{1,2,0:T(2,128)(2,1)S(1)} %reshape.72), channel_id=1, replica_groups=mesh['row'=16,'col'=8] {'col'}, dimensions={0}, use_global_device_ids=true | all-gather | bytes 1152 | tf_op jit(solution)/shard_map/all_gather | solution.py:53
  134.0 0.1 copy.95
  134.0 0.3 copy.97
  134.3 0.3 copy.96
  134.6 0.1 reshape.61
  134.8 0.8 select_reduce_fusion
  135.6 0.2 copy.98
  135.8 0.2 reshape.60
  135.9 119.7 %all-gather.6.cloned.1.call-done = bf16[256,2,128,128]{3,2,1,0:T(8,128)(2,1)} async-done(((bf16[32,2,128,128]{3,2,1,0:T(8,128)(2,1)}), bf16[256,2,128,128]{3,2,1,0:T(8,128)(2,1)}) %all-gather.6.cloned.1.call-update) | async-done | bytes 16777232 | tf_op jit(solution)/shard_map/all_gather | solution.py:52
  255.6 14.2 %copy.104 = bf16[16,8,2,2,128,128]{5,4,3,2,1,0:T(8,128)(2,1)} copy(bf16[16,8,2,2,128,128]{5,4,3,2,0,1:T(8,128)(2,1)} %bitcast.58) | data formatting | bytes 33554432 | tf_op jit(solution)/shard_map/transpose | solution.py:57
  269.8 155.8 %all-gather.4.cloned.1.call-done = bf16[256,2,2,128,128]{4,3,2,1,0:T(8,128)(2,1)} async-done(((bf16[16,2,2,128,128]{4,3,2,1,0:T(8,128)(2,1)}), bf16[256,2,2,128,128]{4,3,2,1,0:T(8,128)(2,1)}) %all-gather.4.cloned.1.call-update) | async-done | bytes 33554448 | tf_op jit(solution)/shard_map/all_gather | solution.py:62
  425.6 59.6 %copy.101 = bf16[256,2,2,128,128]{4,2,1,3,0:T(2,128)(2,1)} copy(bf16[256,2,2,128,128]{4,3,2,1,0:T(8,128)(2,1)} %all-gather.4.cloned.1.call-done) | data formatting | bytes 67108864 | tf_op jit(solution)/shard_map/all_gather | solution.py:62
  485.2 51.3 %convolution_convert_fusion = bf16[256,2,2,128,128]{4,2,3,1,0:T(2,128)(2,1)} fusion(bf16[256,4,128,128,1]{3,1,2,4,0:T(4,128)(2,1)} %bitcast.57, s32[256,4]{1,0:T(8,128)S(1)} %copy.100, s32[256,2,2]{2,1,0:T(2,128)S(1)} %copy.98), kind=kOutput, calls=%fused_computation.1 | convolution fusion | flops 150999040 | bytes 67117056 | tf_op jit(solution)/shard_map/kesf,kftj->kestj/dot_general | solution.py:19
  536.5 37.7 %fusion = f32[256,2,2,128,128]{4,3,2,1,0:T(8,128)} fusion(bf16[256,2,128,128,1]{3,2,4,1,0:T(8,128)(2,1)} %bitcast.56, bf16[256,2,2,128,128]{4,2,3,1,0:T(2,128)(2,1)} %convolution_convert_fusion), kind=kOutput, calls=%fused_computation.2 | convolution fusion | flops 4294967296 | bytes 117440512 | tf_op jit(solution)/shard_map/keti,kestj->kesij/dot_general | solution.py:22
  574.2 65.8 %copy.106 = f32[512,2,128,128]{3,2,1,0:T(8,128)} copy(f32[512,2,128,128]{2,3,1,0:T(8,128)} %bitcast.27) | data formatting | bytes 134217728 | tf_op jit(solution)/shard_map/reshape | solution.py:30
  640.0 6.4 broadcast_in_dim.28
  646.4 150.2 %scatter_fusion = f32[96,2,128,128]{3,2,1,0:T(8,128)} fusion(f32[96,2,128,128]{3,2,1,0:T(8,128)} %broadcast_in_dim.28, s32[512]{0:T(512)S(1)} %bitcast.66, f32[512,2,128,128]{3,2,1,0:T(8,128)} %copy.106), kind=kCustom, calls=%fused_computation | custom fusion | flops 16777216 | bytes 201328640 | tf_op jit(solution)/shard_map/scatter-add | solution.py:32
  (5 shorter events, 0.1 us)
Async XLA Ops:
  6.5 249.1 %all-gather.6.cloned.1.call-start = ((), (), s32[]{:S(2)}) async-start(), calls=%async_computation.5 | async-start | bytes 18874368 | tf_op jit(solution)/shard_map/all_gather | solution.py:52
  75.9 349.7 %all-gather.4.cloned.1.call-start = ((), (), s32[]{:S(2)}) async-start(), calls=%async_computation.4 | async-start | bytes 35651584 | tf_op jit(solution)/shard_map/all_gather | solution.py:62
  78.1 20.9 %all-to-all-start = ((bf16[16,2,2]{2,1,0:T(2,128)(2,1)}), bf16[16,2,2]{2,1,0:T(2,128)(2,1)S(1)}, u32[]{:S(2)}, u32[]{:S(2)}) async-start(bf16[16,2,2]{2,1,0:T(2,128)(2,1)} %convert_element_type.41), calls=%async_computation | async-start | bytes 16384 | tf_op jit(solution)/shard_map/all_to_all | solution.py:45
  100.0 9.4 %all-to-all-start.1 = ((bf16[2,16,2]{2,0,1:T(2,128)(2,1)}), bf16[2,16,2]{2,0,1:T(2,128)(2,1)S(1)}, u32[]{:S(2)}, u32[]{:S(2)}) async-start(bf16[2,16,2]{2,0,1:T(2,128)(2,1)} %bitcast.3), calls=%async_computation.1 | async-start | bytes 16384 | tf_op jit(solution)/shard_map/all_to_all | solution.py:49
Sparse Core Ops, SparseCore 0:
  76.0 179.5 all-gather.5
  257.3 168.2 all-gather.3
where the time goes:
time: 807 us; the launch traced here: 803 us
  waiting for transfers between devices  282 us (35%)
  other arithmetic  152 us (19%)
  local copies, waits for them, and re-layouts  150 us (19%)
  blocking collectives  110 us (14%)
  matrix products  89 us (11%)
  between operations  13.5 us (2%)
    all_gather x1, waiting for transfers between devices, on_device(): b_values = lax.all_gather(x_blocks, 'row', axis=0, tiled=True)  156 us
    scatter-add x1, other arithmetic, reduce_rows(): return zero_sums.at[targets].add(flat)  150 us
    all_gather x1, waiting for transfers between devices, on_device(): lax.all_gather(relaid[0][:, 0], 'col', axis=0, tiled=True)  120 us
    reshape x1, local copies, waits for them, and re-layouts, reduce_rows(): flat = products.reshape(pair_count, kept_count, block_size, block_size)  65.8 us
    all_gather x1, local copies, waits for them, and re-layouts, on_device(): b_values = lax.all_gather(x_blocks, 'row', axis=0, tiled=True)  59.6 us
    dot_general x1, matrix products, block_products(): jnp.einsum('kesf,kftj->kestj', selector, b_flat, preferred_element_type=j...  51.3 us
    dot_general x1, matrix products, block_products(): jnp.einsum('keti,kestj->kesij', a_values, chosen, preferred_element_type=...  37.7 us
    all_to_all x1, blocking collectives, on_device(): lax.all_to_all(x_blocks, 'col', split_axis=0, concat_axis=1, tiled=True)  36.5 us
  transfers between devices with their start and end apart: 4, of which 3 were waited for; matrix products, arithmetic and copies ran while one was open for 2% of the time, Pallas kernels for 0%

commit v1 on v0

v1 whole, which is shorter than its diff:
```python
import functools

import jax
import jax.numpy as jnp
from jax import lax
from jax.experimental import pallas as pl
from jax.experimental.pallas import tpu as pltpu
from jax.sharding import PartitionSpec as P

K_STEP = 32


def match_tables(a_cols, b_cols, kept_columns):
    k_count, slots = a_cols.shape
    width_g = kept_columns.shape[0]
    panel_pos = (lax.broadcasted_iota(jnp.int32, b_cols.shape, 1) * width_g + b_cols).reshape(k_count, -1)
    onehot = a_cols[:, :, None] == lax.broadcasted_iota(jnp.int32, (1, 1, width_g), 2)
    kept_here = jnp.sum(jnp.where(onehot[:, :, :, None], kept_columns[None, None, :, :], 0), axis=2)
    matches = kept_here[:, :, :, None] == panel_pos[:, None, None, :]
    f_index = lax.broadcasted_iota(jnp.int32, matches.shape, 3)
    picked = jnp.sum(jnp.where(matches, f_index, 0), axis=3)
    sel = jnp.where(jnp.any(matches, axis=3), picked, -1)
    return a_cols.reshape(-1).astype(jnp.int32), sel.reshape(-1).astype(jnp.int32)


def products_kernel(rows_ref, sel_ref, a_ref, b_ref, out_ref):
    step = pl.program_id(0)
    k_step = a_ref.shape[0]
    slots = a_ref.shape[1]
    kept = out_ref.shape[1]

    @pl.when(step == 0)
    def _():
        out_ref[...] = jnp.zeros_like(out_ref)

    def body(kk, carry):
        k = step * k_step + kk
        for e in range(slots):
            row = rows_ref[k * slots + e]
            a = a_ref[kk, e]
            for s in range(kept):
                f = sel_ref[(k * slots + e) * kept + s]

                @pl.when(f >= 0)
                def _():
                    b = b_ref[kk, f]
                    out_ref[row, s] += lax.dot_general(
                        a, b, (((0,), (0,)), ((), ())), preferred_element_type=jnp.float32
                    )

        return carry

    lax.fori_loop(0, k_step, body, 0)


def block_products(a_values, b_values, rows, sel, width_g, kept):
    k_count, slots, bs, _ = a_values.shape
    b_flat = b_values.reshape(k_count, -1, bs, bs)
    nb = b_flat.shape[1]
    steps = k_count // K_STEP
    return pl.pallas_call(
        products_kernel,
        out_shape=jax.ShapeDtypeStruct((width_g, kept, bs, bs), jnp.float32),
        grid_spec=pltpu.PrefetchScalarGridSpec(
            num_scalar_prefetch=2,
            grid=(steps,),
            in_specs=[
                pl.BlockSpec((K_STEP, slots, bs, bs), lambda i, r, s: (i, 0, 0, 0)),
                pl.BlockSpec((K_STEP, nb, bs, bs), lambda i, r, s: (i, 0, 0, 0)),
            ],
            out_specs=pl.BlockSpec(
                (width_g, kept, bs, bs), lambda i, r, s: (0, 0, 0, 0), pipeline_mode=pl.Buffered(1)
            ),
        ),
        compiler_params=pltpu.CompilerParams(
            dimension_semantics=("arbitrary",), vmem_limit_bytes=60 * 1024 * 1024
        ),
        cost_estimate=pl.CostEstimate(
            flops=2 * k_count * slots * kept * bs * bs * bs,
            bytes_accessed=(a_values.size + b_values.size) * 2 + width_g * kept * bs * bs * 4,
            transcendentals=0,
        ),
    )(rows, sel, a_values, b_flat)


def on_device(x_blocks, x_columns, kept_columns):
    rows_here = x_blocks.shape[0]
    slot_count = x_blocks.shape[2]
    block_size = x_blocks.shape[-1]
    width_g = kept_columns.shape[0]
    kept = kept_columns.shape[1]
    n_row = lax.axis_size("row")
    n_col = lax.axis_size("col")
    col_tags = x_columns.astype(jnp.bfloat16)
    relaid = (
        lax.all_to_all(x_blocks, "col", split_axis=0, concat_axis=1, tiled=True),
        lax.all_to_all(col_tags, "col", split_axis=0, concat_axis=1, tiled=True),
    )
    relaid = (
        lax.all_to_all(relaid[0], "row", split_axis=1, concat_axis=0, tiled=True),
        lax.all_to_all(relaid[1], "row", split_axis=1, concat_axis=0, tiled=True),
    )
    gathered = (
        lax.all_gather(relaid[0][:, 0], "col", axis=0, tiled=True),
        lax.all_gather(relaid[1][:, 0], "col", axis=0, tiled=True),
    )
    sub_rows = rows_here // n_col
    a_values = gathered[0].reshape(n_col, n_row, sub_rows, slot_count, block_size, block_size)
    a_values = a_values.transpose(1, 0, 2, 3, 4, 5).reshape(
        n_row * rows_here, slot_count, block_size, block_size
    )
    a_cols = gathered[1].reshape(n_col, n_row, sub_rows, slot_count).transpose(1, 0, 2, 3)
    a_cols = a_cols.reshape(n_row * rows_here, slot_count).astype(jnp.int32)
    b_values = lax.all_gather(x_blocks, "row", axis=0, tiled=True)
    b_tags = lax.all_gather(col_tags, "row", axis=0, tiled=True)
    rows, sel = match_tables(a_cols, b_tags.astype(jnp.int32), kept_columns)
    return block_products(a_values, b_values, rows, sel, width_g, kept)


def solution(mesh):
    placed = (P("row", "col", None, None, None), P("row", "col", None), P("row", "col"))
    return jax.shard_map(
        on_device,
        mesh=mesh,
        in_specs=placed,
        out_specs=P("row", "col", None, None),
        check_vma=False,
    )
```

time: 807 us -> 537 us (0.67)
  other arithmetic: 152 us -> 0.89 us
  local copies, waits for them, and re-layouts: 150 us -> 18.9 us
  Pallas kernels: 0 us -> 94.5 us
  matrix products: 89 us -> 0 us
    scatter-add x1 -> x0, other arithmetic: 150 us -> none  [reduce_rows(): return zero_sums.at[targets].add(flat)]
    pallas_call x0 -> x1, Pallas kernels: none -> 94.5 us  [block_products(): pl.pallas_call(products_kernel, out_shape=jax.ShapeDtypeStruct((width_g,...]
    dot_general x2 -> x0, matrix products: 89 us -> none  [the longest x1 51.3 us: block_products(): jnp.einsum('kesf,kftj->kestj', selector, b_flat, preferred_element_type=j...]
    reshape x1 -> x0, local copies, waits for them, and re-layouts: 65.8 us -> none  [reduce_rows(): flat = products.reshape(pair_count, kept_count, block_size, block_size)]
    all_gather x1 -> x0, local copies, waits for them, and re-layouts: 59.6 us -> none  [on_device(): b_values = lax.all_gather(x_blocks, 'row', axis=0, tiled=True)]
  transfers between devices with their start and end apart: 4 -> 4, of which waited for: 3 -> 3; matrix products, arithmetic and copies ran while one was open for 2% -> 4% of each run, Pallas kernels for 0% -> 0%
where the time goes in v1:
time: 537 us; the launch traced here: 527 us
  waiting for transfers between devices  282 us (53%)
  blocking collectives  110 us (20%)
  Pallas kernels  94.5 us (18%)
  local copies, waits for them, and re-layouts  18.9 us (4%)
  between operations  13.5 us (3%)
  starting transfers between devices  6.85 us (1%)
    all_gather x1, waiting for transfers between devices, on_device(): b_values = lax.all_gather(x_blocks, 'row', axis=0, tiled=True)  156 us
    all_gather x1, waiting for transfers between devices, on_device(): lax.all_gather(relaid[0][:, 0], 'col', axis=0, tiled=True)  119 us
    pallas_call x1, Pallas kernels, block_products(): pl.pallas_call(products_kernel, out_shape=jax.ShapeDtypeStruct((width_g,...  94.5 us
    all_to_all x1, blocking collectives, on_device(): lax.all_to_all(x_blocks, 'col', split_axis=0, concat_axis=1, tiled=True)  36.5 us
    all_to_all x1, blocking collectives, on_device(): lax.all_to_all(relaid[0], 'row', split_axis=1, concat_axis=0, tiled=True)  32.4 us
    all_gather x1, blocking collectives, on_device(): lax.all_gather(relaid[1][:, 0], 'col', axis=0, tiled=True)  24.3 us
    all_gather x1, blocking collectives, on_device(): b_tags = lax.all_gather(col_tags, 'row', axis=0, tiled=True)  17.4 us
    transpose x1, local copies, waits for them, and re-layouts, on_device(): a_values.transpose(1, 0, 2, 3, 4, 5)  14.2 us
  transfers between devices with their start and end apart: 4, of which 3 were waited for; matrix products, arithmetic and copies ran while one was open for 4% of the time, Pallas kernels for 0%

profile of v1, /device:TPU:0, one launch (start us, length us, event | category | flops | bytes accessed | tf_op | source)
XLA Modules:
  0.0 526.9 jit_solution(5116509986866759422)
XLA Ops:
  6.5 0.0 all-gather.4.cloned.1.call-start
  6.5 36.5 %all_to_all.66 = bf16[16,2,2,128,128]{4,3,2,1,0:T(8,128)(2,1)S(1)} all-to-all(bf16[16,2,2,128,128]{4,3,2,1,0:T(8,128)(2,1)} %param.3), channel_id=1, replica_groups=mesh['row'=16,'col'=8] {'col'}, dimensions={0} | all-to-all | bytes 4194304 | tf_op jit(solution)/shard_map/all_to_all | solution.py:96
  43.0 0.2 copy.85
  43.2 0.2 copy.86
  43.5 32.4 %all_to_all.67 = bf16[2,16,2,128,128]{4,3,2,0,1:T(8,128)(2,1)} all-to-all(bf16[2,16,2,128,128]{4,3,2,0,1:T(8,128)(2,1)S(1)} %copy.86), channel_id=1, replica_groups=mesh['row'=16,'col'=8] {'row'}, dimensions={1} | all-to-all | bytes 4194304 | tf_op jit(solution)/shard_map/all_to_all | solution.py:100
  75.9 0.0 copy-start
  75.9 0.0 copy-start.1
  75.9 0.0 all-gather.4.cloned.1.call-update
  75.9 0.0 all-gather.6.cloned.1.call-start
  76.0 0.7 all-gather.6.cloned.1.call-update
  76.7 0.0 copy-done
  76.7 0.1 copy.73
  76.8 0.6 convert_element_type.30
  77.4 3.3 all-to-all-start
  80.7 17.4 %all_gather.13 = bf16[256,2,2]{2,1,0:T(2,128)(2,1)S(1)} all-gather(bf16[16,2,2]{2,1,0:T(2,128)(2,1)} %convert_element_type.30), channel_id=1, replica_groups=mesh['row'=16,'col'=8] {'row'}, dimensions={0}, use_global_device_ids=true | all-gather | bytes 2176 | tf_op jit(solution)/shard_map/all_gather | solution.py:115
  98.1 0.1 copy.83
  98.2 0.0 all-to-all-done
  98.2 0.2 copy.89
  98.4 0.8 copy.90
  99.3 3.5 all-to-all-start.1
  102.7 0.1 convert_add_fusion
  102.8 5.8 %all-to-all-done.1 = bf16[2,16,2]{2,0,1:T(2,128)(2,1)S(1)} async-done(((bf16[2,16,2]{2,0,1:T(2,128)(2,1)}), bf16[2,16,2]{2,0,1:T(2,128)(2,1)S(1)}, u32[]{:S(2)}, u32[]{:S(2)}) %all-to-all-start.1) | async-done | bytes 160 | tf_op jit(solution)/shard_map/all_to_all | solution.py:101
  108.7 0.1 copy.77
  108.8 0.1 copy.78
  108.9 0.1 reshape.46
  109.0 24.3 %all-gather = bf16[8,32,2]{1,2,0:T(2,128)(2,1)S(1)} all-gather(bf16[1,32,2]{1,2,0:T(2,128)(2,1)S(1)} %reshape.46), channel_id=1, replica_groups=mesh['row'=16,'col'=8] {'col'}, dimensions={0}, use_global_device_ids=true | all-gather | bytes 1152 | tf_op jit(solution)/shard_map/all_gather | solution.py:105
  133.2 0.1 copy.80
  133.3 0.3 copy.82
  133.6 0.3 copy.81
  133.8 0.1 reshape.43
  134.0 0.0 copy-done.1
  134.0 0.1 select_reduce_fusion
  134.2 0.2 copy.84
  134.4 0.9 select_n.19.sel_ref
  135.3 0.8 reshape.42.rows_ref
  136.1 119.4 %all-gather.4.cloned.1.call-done = bf16[256,2,128,128]{3,2,1,0:T(8,128)(2,1)} async-done(((bf16[32,2,128,128]{3,2,1,0:T(8,128)(2,1)}), bf16[256,2,128,128]{3,2,1,0:T(8,128)(2,1)}) %all-gather.4.cloned.1.call-update) | async-done | bytes 16777232 | tf_op jit(solution)/shard_map/all_gather | solution.py:104
  255.5 14.2 %copy.87 = bf16[16,8,2,2,128,128]{5,4,3,2,1,0:T(8,128)(2,1)} copy(bf16[16,8,2,2,128,128]{5,4,3,2,0,1:T(8,128)(2,1)} %bitcast.36) | data formatting | bytes 33554432 | tf_op jit(solution)/shard_map/transpose | solution.py:109
  269.7 155.8 %all-gather.6.cloned.1.call-done = bf16[256,2,2,128,128]{4,3,2,1,0:T(8,128)(2,1)} async-done(((bf16[16,2,2,128,128]{4,3,2,1,0:T(8,128)(2,1)}), bf16[256,2,2,128,128]{4,3,2,1,0:T(8,128)(2,1)}) %all-gather.6.cloned.1.call-update) | async-done | bytes 33554448 | tf_op jit(solution)/shard_map/all_gather | solution.py:114
  425.5 94.5 %shard_map.37 = f32[96,2,128,128]{3,2,1,0:T(8,128)} custom-call(s32[512]{0:T(512)} %reshape.42.rows_ref, s32[1024]{0:T(1024)} %select_n.19.sel_ref, bf16[256,2,128,128]{3,2,1,0:T(8,128)(2,1)} %bitcast.34, bf16[256,4,128,128]{3,2,1,0:T(8,128)(2,1)} %bitcast.35), custom_call_target="tpu_custom_call" | custom-call | flops 4294967296 | bytes 62914560 | tf_op jit(solution)/shard_map/pallas_call | solution.py:61
  (7 shorter events, 0.1 us)
Async XLA Ops:
  6.5 248.9 %all-gather.4.cloned.1.call-start = ((), (), s32[]{:S(2)}) async-start(), calls=%async_computation.4 | async-start | bytes 18874368 | tf_op jit(solution)/shard_map/all_gather | solution.py:104
  75.9 0.8 copy-start
  75.9 58.1 %copy-start.1 = (s32[96,2]{0,1:T(2,128)S(1)}, s32[96,2]{0,1:T(2,128)}, u32[]{:S(2)}) copy-start(s32[96,2]{0,1:T(2,128)} %param.5) | copy-start | bytes 2308
  75.9 349.6 %all-gather.6.cloned.1.call-start = ((), (), s32[]{:S(2)}) async-start(), calls=%async_computation.5 | async-start | bytes 35651584 | tf_op jit(solution)/shard_map/all_gather | solution.py:114
  77.4 20.8 %all-to-all-start = ((bf16[16,2,2]{2,1,0:T(2,128)(2,1)}), bf16[16,2,2]{2,1,0:T(2,128)(2,1)S(1)}, u32[]{:S(2)}, u32[]{:S(2)}) async-start(bf16[16,2,2]{2,1,0:T(2,128)(2,1)} %convert_element_type.30), calls=%async_computation | async-start | bytes 16384 | tf_op jit(solution)/shard_map/all_to_all | solution.py:97
  99.3 9.4 %all-to-all-start.1 = ((bf16[2,16,2]{2,0,1:T(2,128)(2,1)}), bf16[2,16,2]{2,0,1:T(2,128)(2,1)S(1)}, u32[]{:S(2)}, u32[]{:S(2)}) async-start(bf16[2,16,2]{2,0,1:T(2,128)(2,1)} %bitcast.3), calls=%async_computation.1 | async-start | bytes 16384 | tf_op jit(solution)/shard_map/all_to_all | solution.py:101
Sparse Core Ops, SparseCore 0:
  76.0 179.3 all-gather.3
  257.2 168.2 all-gather.5
